TPU v7x, 256 devices: a whole 4x4x8 slice. The times are simulated.
256 devices in a mesh: pair: 64 (over x, z, core), virt: 4 (over y).
Axes of the slice: x: 4, y: 4, z: 8, core: 2. Of those that a mesh axis runs over, the one named last changes fastest.
Arguments:
- amplitudes: bfloat16 [65536, 8, 1024], P('pair', 'virt'), may hold values from -6 to 6
- tile_mask: int32 [65536, 8], P('pair', 'virt'), may hold values from 0 to 1
- integrals: bfloat16 [8, 1024, 1024], P('virt', 'pair'), may hold values from -0.0625 to 0.0625
- pair_energy: float32 [65536], P(('pair', 'virt')), may hold values from -2 to -0.5
- virt_energy: float32 [1024], replicated, may hold values from 0.5 to 3
Outputs:
- update: bfloat16 [65536, 1024], P(('pair', 'virt'))
All inputs are finite; a program needn't handle non-finite values.
Results may differ from a plain program's by a relative error of at most 0.011.
Values may be sent and summed in bfloat16 or wider, within the bound.
A program may use at most 64 MiB of HBM per device.

v0:
```python
import jax
import jax.numpy as jnp
from jax import lax
from jax.sharding import PartitionSpec as P


def on_device(amplitudes, tile_mask, integrals, pair_energy, virt_energy):
    masked = amplitudes * tile_mask.astype(jnp.bfloat16)[:, :, None]
    partial_value = jnp.einsum(
        "ptk,tkn->pn",
        masked,
        lax.all_gather(integrals, "pair", axis=1, tiled=True),
        preferred_element_type=jnp.float32,
    )
    ladder = lax.psum_scatter(
        partial_value.astype(jnp.bfloat16), "virt", scatter_dimension=0, tiled=True
    ).astype(jnp.float32)
    denom = virt_energy[None, :] - pair_energy[:, None]
    return (ladder / denom).astype(jnp.bfloat16)


def solution(mesh):
    placed = (
        P("pair", "virt", None),
        P("pair", "virt"),
        P("virt", "pair", None),
        P(("pair", "virt")),
        P(),
    )
    return jax.shard_map(
        on_device, mesh=mesh, in_specs=placed, out_specs=P(("pair", "virt"), None), check_vma=False
    )
```

profile of v0, /device:TPU:1, one launch (start us, length us, event | category | flops | bytes accessed | tf_op | source)
XLA Modules:
  0.0 140.7 jit_solution(15998661899004031293)
XLA Ops:
  6.5 0.0 all-gather.2.cloned.1.call-start
  6.5 0.7 all-gather.2.cloned.1.call-update
  7.3 0.0 reduce-scatter.2.cloned.1.call-start
  7.3 0.7 convert_element_type.12
  8.0 0.2 copy.6
  8.2 8.0 %broadcast_multiply_fusion = bf16[1024,2,1024]{2,1,0:T(2,128)(2,1)} fusion(bf16[1024,2,1024]{2,1,0:T(2,128)(2,1)} %param.5, bf16[1024,2]{1,0:T(8,128)(2,1)S(1)} %copy.6), kind=kLoop, calls=%fused_computation.3 | loop fusion | flops 2097152 | bytes 8392704 | tf_op jit(solution)/shard_map/mul | solution.py:8
  16.2 0.0 copy-start
  16.2 0.0 copy-start.1
  16.2 77.1 %all-gather.2.cloned.1.call-done = bf16[2,1024,1024]{2,1,0:T(8,128)(2,1)} async-done(((bf16[2,16,1024]{2,1,0:T(8,128)(2,1)}), bf16[2,1024,1024]{2,1,0:T(8,128)(2,1)}) %all-gather.2.cloned.1.call-update) | async-done | bytes 4194320 | tf_op jit(solution)/shard_map/all_gather | solution.py:12
  93.3 9.3 %bitcast_convert_fusion = bf16[1024,1024]{1,0:T(8,128)(2,1)} fusion(bf16[2,1024,1024]{2,1,0:T(8,128)(2,1)} %all-gather.2.cloned.1.call-done, bf16[1024,2,1024]{2,1,0:T(2,128)(2,1)} %broadcast_multiply_fusion), kind=kOutput, calls=%fused_computation | convolution fusion | flops 4296015872 | bytes 10485760 | tf_op jit(solution)/shard_map/ptk,tkn->pn/dot_general | solution.py:9
  102.6 0.0 reduce-scatter.2.cloned.1.call-update
  102.7 29.1 %reduce-scatter.2.cloned.1.call-done = bf16[256,1024]{1,0:T(8,128)(2,1)} async-done(((bf16[1024,1024]{1,0:T(8,128)(2,1)}), bf16[256,1024]{1,0:T(8,128)(2,1)}) %reduce-scatter.2.cloned.1.call-update) | async-done | bytes 524304 | tf_op jit(solution)/shard_map/reduce_scatter | solution.py:15
  131.8 0.0 copy-done
  131.8 0.0 copy-done.1
  131.8 2.1 %divide_convert_fusion = bf16[256,1024]{1,0:T(8,128)(2,1)} fusion(bf16[256,1024]{1,0:T(8,128)(2,1)} %reduce-scatter.2.cloned.1.call-done, f32[256]{0:T(256)S(1)} %copy-done.1, f32[1024]{0:T(1024)S(1)} %copy-done), kind=kLoop, calls=%fused_computation.4 | loop fusion | flops 1048576 | bytes 1053696 | tf_op jit(solution)/shard_map/convert_element_type | solution.py:19
Async XLA Ops:
  6.5 86.8 %all-gather.2.cloned.1.call-start = ((), (), s32[]{:S(2)}) async-start(), calls=%async_computation.1 | async-start | bytes 4259840 | tf_op jit(solution)/shard_map/all_gather | solution.py:12
  7.3 124.5 %reduce-scatter.2.cloned.1.call-start = ((), (), s32[]{:S(2)}) async-start(), calls=%async_computation.2 | async-start | bytes 2621440 | tf_op jit(solution)/shard_map/reduce_scatter | solution.py:15
  16.2 115.6 %copy-start = (f32[1024]{0:T(1024)S(1)}, f32[1024]{0:T(1024)}, u32[]{:S(2)}) copy-start(f32[1024]{0:T(1024)} %param.9) | copy-start | bytes 12292
  16.2 115.6 %copy-start.1 = (f32[256]{0:T(256)S(1)}, f32[256]{0:T(256)}, u32[]{:S(2)}) copy-start(f32[256]{0:T(256)} %param.8) | copy-start | bytes 3076
Sparse Core Ops, SparseCore 0:
  10.1 83.1 all-gather.1
  102.8 28.9 reduce-scatter.1
where the time goes:
time: 141 us
  waiting for transfers between devices  107 us (76%)
  between operations  13.4 us (10%)
  other arithmetic  10.8 us (8%)
  matrix products  9.32 us (7%)
    all_gather x1, waiting for transfers between devices, on_device(): lax.all_gather(integrals, 'pair', axis=1, tiled=True)  77.1 us
    reduce_scatter x1, waiting for transfers between devices, on_device(): lax.psum_scatter(partial_value.astype(jnp.bfloat16), 'virt', scatter_dime...  29.1 us
    dot_general x1, matrix products, on_device(): jnp.einsum('ptk,tkn->pn', masked, lax.all_gather(integrals, 'pair', axis=...  9.32 us
    mul x1, other arithmetic, on_device(): masked = amplitudes * tile_mask.astype(jnp.bfloat16)[:, :, None]  8.03 us
  transfers between devices with their start and end apart: 2, of which 2 were waited for; matrix products, arithmetic and copies ran while one was open for 6% of the time, Pallas kernels for 0%

commit v1 on v0

--- a/solution.py
+++ b/solution.py
@@ -2,6 +2,13 @@
 import jax.numpy as jnp
 from jax import lax
 from jax.sharding import PartitionSpec as P
+
+
+def all_by_exchange(value, name, d):
+    peers = lax.axis_size(name)
+    tiles = jnp.stack([value for _ in range(peers)])
+    tiles = lax.all_to_all(tiles, name, split_axis=0, concat_axis=0)
+    return jnp.concatenate(tiles, axis=d)
 
 
 def on_device(amplitudes, tile_mask, integrals, pair_energy, virt_energy):
@@ -9,7 +16,7 @@
     partial_value = jnp.einsum(
         "ptk,tkn->pn",
         masked,
-        lax.all_gather(integrals, "pair", axis=1, tiled=True),
+        all_by_exchange(integrals, "pair", 1),
         preferred_element_type=jnp.float32,
     )
     ladder = lax.psum_scatter(

time: 141 us -> 167 us (1.18)
  starting transfers between devices: 0.04 us -> 13.3 us
  waiting for transfers between devices: 107 us -> 117 us
  local copies, waits for them, and re-layouts: 0.21 us -> 7 us
  matrix products: 9.32 us -> 5.9 us
    all_to_all x0 -> x1, waiting for transfers between devices: none -> 87.6 us  [all_by_exchange(): tiles = lax.all_to_all(tiles, name, split_axis=0, concat_axis=0)]
    all_gather x1 -> x0, waiting for transfers between devices: 77.1 us -> none  [on_device(): lax.all_gather(integrals, 'pair', axis=1, tiled=True)]
    all_to_all x0 -> x1, starting transfers between devices: none -> 13.3 us  [all_by_exchange(): tiles = lax.all_to_all(tiles, name, split_axis=0, concat_axis=0)]
    dot_general x1, matrix products: 9.32 us -> 5.9 us  [on_device(): jnp.einsum('ptk,tkn->pn', masked, all_by_exchange(integrals, 'pair', 1),...]
    another operation x0 -> x1, local copies, waits for them, and re-layouts: none -> 3.34 us  [all_by_exchange(): tiles = jnp.stack([value for _ in range(peers)])]
    reshape x0 -> x1, local copies, waits for them, and re-layouts: none -> 2.8 us  [all_by_exchange(): return jnp.concatenate(tiles, axis=d)]
  transfers between devices with their start and end apart: 2 -> 2, of which waited for: 2 -> 2; matrix products, arithmetic and copies ran while one was open for 6% -> 5% of each run, Pallas kernels for 0% -> 0%
where the time goes in v1:
time: 167 us; the launch traced here: 166 us
  waiting for transfers between devices  117 us (70%)
  between operations  13.4 us (8%)
  starting transfers between devices  13.3 us (8%)
  other arithmetic  10.1 us (6%)
  local copies, waits for them, and re-layouts  7 us (4%)
  matrix products  5.9 us (4%)
    all_to_all x1, waiting for transfers between devices, all_by_exchange(): tiles = lax.all_to_all(tiles, name, split_axis=0, concat_axis=0)  87.6 us
    reduce_scatter x1, waiting for transfers between devices, on_device(): lax.psum_scatter(partial_value.astype(jnp.bfloat16), 'virt', scatter_dime...  29 us
    all_to_all x1, starting transfers between devices, all_by_exchange(): tiles = lax.all_to_all(tiles, name, split_axis=0, concat_axis=0)  13.3 us
    mul x1, other arithmetic, on_device(): masked = amplitudes * tile_mask.astype(jnp.bfloat16)[:, :, None]  8.02 us
    dot_general x1, matrix products, on_device(): jnp.einsum('ptk,tkn->pn', masked, all_by_exchange(integrals, 'pair', 1),...  5.9 us
    another operation x1, local copies, waits for them, and re-layouts, all_by_exchange(): tiles = jnp.stack([value for _ in range(peers)])  3.34 us
  transfers between devices with their start and end apart: 2, of which 2 were waited for; matrix products, arithmetic and copies ran while one was open for 5% of the time, Pallas kernels for 0%

profile of v1, /device:TPU:1, one launch (start us, length us, event | category | flops | bytes accessed | tf_op | source)
XLA Modules:
  0.0 166.3 jit_solution(2286762615034849401)
XLA Ops:
  6.5 3.3 %stack.2 = bf16[64,2,16,1024]{3,2,1,0:T(8,128)(2,1)} broadcast(bf16[2,16,1024]{2,1,0:T(8,128)(2,1)} %param.7), dimensions={1,2,3} | broadcast | bytes 4259840 | tf_op jit(solution)/shard_map/stack | solution.py:9
  9.9 0.0 copy-start.1
  9.9 13.3 %all-to-all-start = ((bf16[64,2,16,1024]{3,2,1,0:T(8,128)(2,1)}), bf16[64,2,16,1024]{3,2,1,0:T(8,128)(2,1)}, u32[]{:S(2)}, u32[]{:S(2)}) async-start(bf16[64,2,16,1024]{3,2,1,0:T(8,128)(2,1)} %stack.2), calls=%async_computation | async-start | bytes 8388608 | tf_op jit(solution)/shard_map/all_to_all | solution.py:10
  23.2 0.0 reduce-scatter.2.cloned.1.call-start
  23.2 0.0 copy-done.1
  23.3 0.2 copy.8
  23.5 8.0 %broadcast_multiply_fusion = bf16[1024,2,1024]{2,1,0:T(2,128)(2,1)} fusion(bf16[1024,2,1024]{2,1,0:T(2,128)(2,1)} %param.5, bf16[1024,2]{1,0:T(8,128)(2,1)S(1)} %copy.8), kind=kLoop, calls=%fused_computation.3 | loop fusion | flops 2097152 | bytes 8392704 | tf_op jit(solution)/shard_map/mul | solution.py:15
  31.5 87.6 %all-to-all-done = bf16[64,2,16,1024]{3,2,1,0:T(8,128)(2,1)} async-done(((bf16[64,2,16,1024]{3,2,1,0:T(8,128)(2,1)}), bf16[64,2,16,1024]{3,2,1,0:T(8,128)(2,1)}, u32[]{:S(2)}, u32[]{:S(2)}) %all-to-all-start) | async-done | bytes 4194336 | tf_op jit(solution)/shard_map/all_to_all | solution.py:10
  119.0 0.0 copy-start
  119.0 2.8 %copy.9 = bf16[2,64,16,1024]{3,2,1,0:T(8,128)(2,1)S(1)} copy(bf16[2,64,16,1024]{3,2,0,1:T(8,128)(2,1)} %bitcast) | data formatting | bytes 8388608 | tf_op jit(solution)/shard_map/reshape | solution.py:11
  121.8 0.6 copy-done
  122.5 0.0 copy-start.2
  122.5 0.0 copy-start.3
  122.5 5.9 %bitcast_convert_fusion = bf16[1024,1024]{1,0:T(8,128)(2,1)} fusion(bf16[2,1024,1024]{2,1,0:T(8,128)(2,1)S(1)} %bitcast.5, bf16[1024,2,1024]{2,1,0:T(2,128)(2,1)S(1)} %copy-done), kind=kOutput, calls=%fused_computation | convolution fusion | flops 4296015872 | bytes 10485760 | tf_op jit(solution)/shard_map/ptk,tkn->pn/dot_general | solution.py:16
  128.4 0.0 reduce-scatter.2.cloned.1.call-update
  128.4 29.0 %reduce-scatter.2.cloned.1.call-done = bf16[256,1024]{1,0:T(8,128)(2,1)} async-done(((bf16[1024,1024]{1,0:T(8,128)(2,1)}), bf16[256,1024]{1,0:T(8,128)(2,1)}) %reduce-scatter.2.cloned.1.call-update) | async-done | bytes 524304 | tf_op jit(solution)/shard_map/reduce_scatter | solution.py:22
  157.4 0.0 copy-done.2
  157.4 0.0 copy-done.3
  157.4 2.1 %divide_convert_fusion = bf16[256,1024]{1,0:T(8,128)(2,1)} fusion(bf16[256,1024]{1,0:T(8,128)(2,1)} %reduce-scatter.2.cloned.1.call-done, f32[256]{0:T(256)S(1)} %copy-done.3, f32[1024]{0:T(1024)S(1)} %copy-done.2), kind=kLoop, calls=%fused_computation.4 | loop fusion | flops 1048576 | bytes 1053696 | tf_op jit(solution)/shard_map/convert_element_type | solution.py:26
  (1 shorter events, 0.0 us)
Async XLA Ops:
  9.9 13.4 %copy-start.1 = (s32[1024,2]{0,1:T(2,128)S(1)}, s32[1024,2]{0,1:T(2,128)}, u32[]{:S(2)}) copy-start(s32[1024,2]{0,1:T(2,128)} %param.6) | copy-start | bytes 24580
  9.9 109.2 %all-to-all-start = ((bf16[64,2,16,1024]{3,2,1,0:T(8,128)(2,1)}), bf16[64,2,16,1024]{3,2,1,0:T(8,128)(2,1)}, u32[]{:S(2)}, u32[]{:S(2)}) async-start(bf16[64,2,16,1024]{3,2,1,0:T(8,128)(2,1)} %stack.2), calls=%async_computation | async-start | bytes 8388608 | tf_op jit(solution)/shard_map/all_to_all | solution.py:10
  23.2 134.2 %reduce-scatter.2.cloned.1.call-start = ((), (), s32[]{:S(2)}) async-start(), calls=%async_computation.2 | async-start | bytes 2621440 | tf_op jit(solution)/shard_map/reduce_scatter | solution.py:22
  119.0 3.4 %copy-start = (bf16[1024,2,1024]{2,1,0:T(2,128)(2,1)S(1)}, bf16[1024,2,1024]{2,1,0:T(2,128)(2,1)}, u32[]{:S(2)}) copy-start(bf16[1024,2,1024]{2,1,0:T(2,128)(2,1)} %broadcast_multiply_fusion) | copy-start | bytes 12582916
  122.5 34.9 %copy-start.2 = (f32[1024]{0:T(1024)S(1)}, f32[1024]{0:T(1024)}, u32[]{:S(2)}) copy-start(f32[1024]{0:T(1024)} %param.9) | copy-start | bytes 12292
  122.5 34.9 %copy-start.3 = (f32[256]{0:T(256)S(1)}, f32[256]{0:T(256)}, u32[]{:S(2)}) copy-start(f32[256]{0:T(256)} %param.8) | copy-start | bytes 3076
Sparse Core Ops, SparseCore 0:
  128.5 28.8 reduce-scatter.1
